TPU v7x, 512 devices: a whole 4x8x8 slice. The times are simulated.
512 devices in a mesh: tok: 32 (over y, x), exp: 16 (over z, core).
Axes of the slice: x: 4, y: 8, z: 8, core: 2. Of those that a mesh axis runs over, the one named last changes fastest.
Arguments:
- tokens: bfloat16 [512, 6144], P('tok', 'exp'), may hold values from -6 to 6
- route_ids: int32 [512, 2], P('tok'), may hold values from 0 to 3, all different within a row; in each aligned block of 16 rows (0 to 15, 16 to 31, ...) at most 12 rows name the same one
- gate_codes: int32 [512, 2], P('tok'), may hold values from 1 to 255
- merge_labels: int32 [4], replicated, may hold values from 0 to 1, as said below
- freq_counts: int32 [4], replicated, may hold values from 1024 to 4096
- w_gate: bfloat16 [32768, 6144], P(('tok', 'exp')), may hold values from -0.078125 to 0.078125
- w_up: bfloat16 [32768, 6144], P(('tok', 'exp')), may hold values from -0.078125 to 0.078125
- w_down: bfloat16 [32768, 6144], P('tok', 'exp'), may hold values from -0.0625 to 0.0625
Outputs:
- initial_out: bfloat16 [512, 6144], P('tok', 'exp')
- merged_out: bfloat16 [512, 6144], P('tok', 'exp')
Inputs may be any that keep to these rules, and one draw needn't show every extreme that they name: `route_ids`: the 2 ids of a row differ. Among the 16 rows of one token shard no expert is named more than 12 times, a bound that some block reaches. `merge_labels`: experts with equal labels form one merge group; every group has exactly two experts.
All inputs are finite; a program needn't handle non-finite values.
Results may differ from a plain program's by a relative error of at most 0.0085.
Values may be sent and summed in bfloat16 or wider, within the bound.
A program may use at most 64 MiB of HBM per device.

v0:
```python
import jax
import jax.numpy as jnp
from jax import lax
from jax.sharding import PartitionSpec as P

EXPERTS = 4
TOP = 2
CAP = 12


def passed_along(value, axis, by):
    devices = lax.axis_size(axis)
    return lax.ppermute(value, axis, [(i, (i + by) % devices) for i in range(devices)])


def local(tokens, route_ids, gate_codes, merge_labels, freq_counts, w_gate, w_up, w_down):
    n_tok = lax.axis_size("tok")
    span = n_tok // EXPERTS
    expert = lax.axis_index("tok") // span
    tok_dev = tokens.shape[0]
    width = tokens.shape[1]
    flat = route_ids.reshape(-1)
    labels_idx = jnp.arange(EXPERTS, dtype=jnp.int32)
    picked = (flat[:, None] == labels_idx[None, :]).astype(jnp.int32)
    before = jnp.cumsum(picked, axis=0) - picked
    slot = jnp.sum(before * picked, axis=1)
    places = jnp.arange(CAP, dtype=jnp.int32)
    landing = picked.T[:, None, :] * (slot[None, None, :] == places[None, :, None]).astype(
        jnp.int32
    )
    landing = landing.reshape(EXPERTS, CAP, tok_dev, TOP)
    scale = gate_codes.astype(jnp.float32) / 256.0
    place_map = jnp.sum(landing, axis=3).astype(jnp.bfloat16)
    weighted = jnp.sum(landing.astype(jnp.float32) * scale[None, None, :, :], axis=3)
    packed = jnp.einsum(
        "ecn,nd->ecd", place_map, tokens, preferred_element_type=jnp.float32
    ).astype(jnp.bfloat16)
    copies = jnp.repeat(packed, span, axis=0)
    arrived = lax.all_to_all(copies, "tok", split_axis=0, concat_axis=0, tiled=True)
    rows_part = arrived.reshape(n_tok * CAP, width)
    rows = lax.all_gather(rows_part, "exp", axis=1, tiled=True)

    def project(gate_w, up_w, down_w):
        gate = jnp.einsum("sd,fd->sf", rows, gate_w, preferred_element_type=jnp.float32)
        upper = jnp.einsum("sd,fd->sf", rows, up_w, preferred_element_type=jnp.float32)
        hidden = (jax.nn.silu(gate) * upper).astype(jnp.bfloat16)
        units = lax.all_gather(hidden, "exp", axis=1, tiled=True)
        return jnp.dot(units, down_w, preferred_element_type=jnp.float32)

    first = project(w_gate, w_up, w_down)
    freq = freq_counts.astype(jnp.float32)
    own_label = jnp.sum(jnp.where(labels_idx == expert, merge_labels, 0))
    member = jnp.where(merge_labels == own_label, freq, jnp.float32(0.0))
    coef = member / jnp.sum(member)

    def weight_of(source):
        return jnp.sum(jnp.where(labels_idx == source, coef, jnp.float32(0.0)))

    own_weight = weight_of(expert)
    accums = (
        own_weight * w_gate.astype(jnp.float32),
        own_weight * w_up.astype(jnp.float32),
        own_weight * w_down.astype(jnp.float32),
    )
    for offset in range(1, EXPERTS):
        peers = passed_along((w_gate, w_up, w_down), "tok", offset * span)
        factor = weight_of((expert - offset) % EXPERTS)
        accums = (
            accums[0] + factor * peers[0].astype(jnp.float32),
            accums[1] + factor * peers[1].astype(jnp.float32),
            accums[2] + factor * peers[2].astype(jnp.float32),
        )
    second = project(
        accums[0].astype(jnp.bfloat16),
        accums[1].astype(jnp.bfloat16),
        accums[2].astype(jnp.bfloat16),
    )
    stacked = jnp.stack(
        [first.reshape(n_tok, CAP, width), second.reshape(n_tok, CAP, width)], axis=0
    )
    backs = lax.all_to_all(
        stacked.astype(jnp.bfloat16), "tok", split_axis=1, concat_axis=1, tiled=True
    ).astype(stacked.dtype)
    totals = jnp.sum(backs.reshape(2, EXPERTS, span, CAP, width), axis=2)
    final = jnp.einsum(
        "ecn,xecd->xnd",
        weighted,
        totals,
        precision=lax.Precision.HIGHEST,
        preferred_element_type=jnp.float32,
    )
    return (final[0].astype(jnp.bfloat16), final[1].astype(jnp.bfloat16))


def solution(mesh):
    return jax.shard_map(
        local,
        mesh=mesh,
        in_specs=(
            P("tok", "exp"),
            P("tok", None),
            P("tok", None),
            P(),
            P(),
            P(("tok", "exp"), None),
            P(("tok", "exp"), None),
            P("tok", "exp"),
        ),
        out_specs=(P("tok", "exp"), P("tok", "exp")),
        check_vma=False,
    )
```

profile of v0, /device:TPU:8, one launch (start us, length us, event | category | flops | bytes accessed | tf_op | source)
XLA Modules:
  0.0 296.3 jit_solution(11261646485899905770)
XLA Ops:
  7.2 0.0 copy-start
  7.2 0.0 copy-start.2
  7.2 0.0 copy-start.3
  7.2 0.0 all-gather.2.cloned.1.call-start
  7.3 0.8 fusion.23
  8.1 0.8 copy.25
  8.8 0.1 eq.85
  8.9 0.1 fusion.21
  9.0 0.1 reduce_window_sum.11
  9.0 0.2 select_reduce_fusion
  9.2 0.1 eq.89
  9.3 0.1 copy.26
  9.5 0.0 copy-done
  9.5 0.1 convolution_convert_fusion.2
  9.6 24.7 %all_to_all.10 = bf16[32,12,384]{2,1,0:T(8,128)(2,1)S(1)} all-to-all(bf16[32,12,384]{2,1,0:T(8,128)(2,1)S(1)} %bitcast.34), channel_id=1, replica_groups=mesh['tok'=32,'exp'=16] {'tok'}, dimensions={0} | all-to-all | bytes 589824 | tf_op jit(solution)/shard_map/all_to_all | solution.py:39
  34.3 0.8 reshape.75
  35.1 0.0 all-gather.2.cloned.1.call-update
  35.1 2.9 collective-permute-start
  38.0 5.1 %collective-permute-start.2 = (bf16[64,6144]{1,0:T(8,128)(2,1)S(1)}, bf16[64,6144]{1,0:T(8,128)(2,1)}, u32[]{:S(2)}, u32[]{:S(2)}) collective-permute-start(bf16[64,6144]{1,0:T(8,128)(2,1)S(1)} %copy-done.2), channel_id=1, source_target_pairs={{0,384},{16,400},{32,416},{48,432},{64,448},{80,464},{96,480},{112... | collective-permute-start | bytes 2359304 | tf_op jit(solution)/shard_map/ppermute | solution.py:13
  43.1 3.3 %collective-permute-start.1 = (bf16[64,6144]{1,0:T(8,128)(2,1)S(1)}, bf16[64,6144]{1,0:T(8,128)(2,1)}, u32[]{:S(2)}, u32[]{:S(2)}) collective-permute-start(bf16[64,6144]{1,0:T(8,128)(2,1)S(1)} %copy-done.2), channel_id=1, source_target_pairs={{0,256},{16,272},{32,288},{48,304},{64,320},{80,336},{96,352},{112... | collective-permute-start | bytes 2359304 | tf_op jit(solution)/shard_map/ppermute | solution.py:13
  46.5 2.9 collective-permute-start.3
  49.3 5.1 %collective-permute-start.5 = (bf16[64,6144]{1,0:T(8,128)(2,1)S(1)}, bf16[64,6144]{1,0:T(8,128)(2,1)}, u32[]{:S(2)}, u32[]{:S(2)}) collective-permute-start(bf16[64,6144]{1,0:T(8,128)(2,1)S(1)} %copy-done.3), channel_id=1, source_target_pairs={{0,384},{16,400},{32,416},{48,432},{64,448},{80,464},{96,480},{112... | collective-permute-start | bytes 2359304 | tf_op jit(solution)/shard_map/ppermute | solution.py:13
  54.5 0.6 fusion.24
  55.1 0.0 copy-done.4
  55.1 1.2 fusion.29
  56.4 2.0 fusion.25
  58.4 22.8 %all-gather.2.cloned.1.call-done = bf16[384,6144]{1,0:T(8,128)(2,1)} async-done(((bf16[384,384]{1,0:T(8,128)(2,1)}), bf16[384,6144]{1,0:T(8,128)(2,1)}) %all-gather.2.cloned.1.call-update) | async-done | bytes 4718608 | tf_op jit(solution)/shard_map/all_gather | solution.py:41
  81.2 4.0 %fusion.30 = f32[384,64]{0,1:T(8,128)S(1)} fusion(bf16[384,6144]{1,0:T(8,128)(2,1)} %all-gather.2.cloned.1.call-done, bf16[64,6144]{1,0:T(8,128)(2,1)S(1)} %copy-done.2), kind=kOutput, calls=%fused_computation.57 | convolution fusion | flops 301989888 | bytes 5603328 | tf_op jit(solution)/shard_map/sd,fd->sf/dot_general | solution.py:44
  85.3 0.0 copy-start.7
  85.3 1.6 fusion
  86.9 18.0 %all_gather.10 = bf16[384,1024]{0,1:T(8,128)(2,1)S(1)} all-gather(bf16[384,64]{0,1:T(8,128)(2,1)S(1)} %fusion), channel_id=1, replica_groups=mesh['tok'=32,'exp'=16] {'exp'}, dimensions={1}, use_global_device_ids=true | all-gather | bytes 835584 | tf_op jit(solution)/shard_map/all_gather | solution.py:47
  104.9 0.0 collective-permute-done
  104.9 6.5 %collective-permute-start.4 = (bf16[64,6144]{1,0:T(8,128)(2,1)S(1)}, bf16[64,6144]{1,0:T(8,128)(2,1)}, u32[]{:S(2)}, u32[]{:S(2)}) collective-permute-start(bf16[64,6144]{1,0:T(8,128)(2,1)S(1)} %copy-done.3), channel_id=1, source_target_pairs={{0,256},{16,272},{32,288},{48,304},{64,320},{80,336},{96,352},{112... | collective-permute-start | bytes 2359304 | tf_op jit(solution)/shard_map/ppermute | solution.py:13
  111.4 0.0 copy-done.7
  111.4 0.6 convolution_convert_fusion.1
  112.0 0.0 slice-start
  112.0 0.1 stack_reshape.8
  112.1 0.0 collective-permute-done.2
  112.1 2.6 collective-permute-start.6
  114.7 0.0 collective-permute-done.1
  114.7 5.5 %collective-permute-start.8 = (bf16[1024,384]{1,0:T(8,128)(2,1)}, bf16[1024,384]{1,0:T(8,128)(2,1)S(1)}, u32[]{:S(2)}, u32[]{:S(2)}) collective-permute-start(bf16[1024,384]{1,0:T(8,128)(2,1)} %param.15), channel_id=1, source_target_pairs={{0,384},{16,400},{32,416},{48,432},{64,448},{80,464},{96,480},{112... | collective-permute-start | bytes 2359304 | tf_op jit(solution)/shard_map/ppermute | solution.py:13
  120.2 0.0 copy-start.8
  120.2 0.0 slice-start.1
  120.2 7.7 %fusion.3 = f32[384,64]{0,1:T(8,128)S(1)} fusion(bf16[384,6144]{1,0:T(8,128)(2,1)} %all-gather.2.cloned.1.call-done, bf16[64,6144]{1,0:T(8,128)(2,1)} %collective-permute-done.2, bf16[64,6144]{1,0:T(8,128)(2,1)} %collective-permute-done.1, bf16[64,6144]{1,0:T(8,128)(2,1)} %collective-permute-done, bf16[64,6144]{1,0:T(8,128)(2,1)S(1)} %copy-done.2, ...), kind=kOutput, calls=%fused_computation.12 | convolution fusion | flops 306708480 | bytes 7962640 | tf_op jit(solution)/shard_map/sd,fd->sf/dot_general | solution.py:44
  127.9 88.3 %collective-permute-done.3 = bf16[64,6144]{1,0:T(8,128)(2,1)} collective-permute-done((bf16[64,6144]{1,0:T(8,128)(2,1)S(1)}, bf16[64,6144]{1,0:T(8,128)(2,1)}, u32[]{:S(2)}, u32[]{:S(2)}) %collective-permute-start.3) | collective-permute-done | bytes 786464 | tf_op jit(solution)/shard_map/ppermute | solution.py:13
  216.3 1.9 collective-permute-start.7
  218.2 0.0 collective-permute-done.5
  218.2 0.0 collective-permute-done.4
  218.2 5.9 %multiply_convert_fusion = bf16[384,64]{0,1:T(8,128)(2,1)S(1)} fusion(f32[384,64]{0,1:T(8,128)S(1)} %fusion.3, bf16[384,6144]{1,0:T(8,128)(2,1)S(1)} %bitcast.33, bf16[64,6144]{1,0:T(8,128)(2,1)} %collective-permute-done.5, bf16[64,6144]{1,0:T(8,128)(2,1)} %collective-permute-done.4, bf16[64,6144]{1,0:T(8,128)(2,1)} %collective-permute-done.3, ...), kind=kOutput, calls=%fused_computation.27 | convolution fusion | flops 306855936 | bytes 8011792 | tf_op jit(solution)/shard_map/sd,fd->sf/dot_general | solution.py:45
  224.1 16.8 %all_gather.11 = bf16[384,1024]{0,1:T(8,128)(2,1)S(1)} all-gather(bf16[384,64]{0,1:T(8,128)(2,1)S(1)} %multiply_convert_fusion), channel_id=1, replica_groups=mesh['tok'=32,'exp'=16] {'exp'}, dimensions={1}, use_global_device_ids=true | all-gather | bytes 835584 | tf_op jit(solution)/shard_map/all_gather | solution.py:47
  241.0 0.0 collective-permute-done.6
  241.0 0.0 collective-permute-done.8
  241.0 4.5 %collective-permute-done.7 = bf16[1024,384]{1,0:T(8,128)(2,1)S(1)} collective-permute-done((bf16[1024,384]{1,0:T(8,128)(2,1)S(1)}, bf16[1024,384]{1,0:T(8,128)(2,1)S(1)}, u32[]{:S(2)}, u32[]{:S(2)}) %collective-permute-start.7) | collective-permute-done | bytes 786464 | tf_op jit(solution)/shard_map/ppermute | solution.py:13
  245.4 3.5 %convolution_convert_fusion = bf16[384,384]{1,0:T(8,128)(2,1)S(1)} fusion(bf16[384,1024]{0,1:T(8,128)(2,1)S(1)} %all_gather.11, bf16[1024,384]{1,0:T(8,128)(2,1)S(1)} %collective-permute-done.8, bf16[1024,384]{1,0:T(8,128)(2,1)S(1)} %collective-permute-done.7, bf16[1024,384]{1,0:T(8,128)(2,1)S(1)} %collective-permute-done.6, ...), kind=kOutput, calls=%fused_computation.3 | convolution fusion | flops 306855936 | bytes 4227088 | tf_op jit(solution)/shard_map/dot_general | solution.py:48
  249.0 0.1 stack_reshape.9
  249.1 0.2 pad_maximum_fusion
  249.2 0.0 copy-start.6
  249.2 1.4 copy.28
  250.6 20.4 %all-to-all-start.1 = ((bf16[2,32,12,384]{3,0,2,1:T(2,128)(2,1)}), bf16[2,32,12,384]{3,0,2,1:T(2,128)(2,1)S(1)}, u32[]{:S(2)}, u32[]{:S(2)}) async-start(bf16[2,32,12,384]{3,0,2,1:T(2,128)(2,1)} %copy.28), calls=%async_computation.1 | async-start | bytes 1179648 | tf_op jit(solution)/shard_map/all_to_all | solution.py:81
  271.1 0.1 copy.30
  271.2 16.8 %all-to-all-done.1 = bf16[2,32,12,384]{3,0,2,1:T(2,128)(2,1)S(1)} async-done(((bf16[2,32,12,384]{3,0,2,1:T(2,128)(2,1)}), bf16[2,32,12,384]{3,0,2,1:T(2,128)(2,1)S(1)}, u32[]{:S(2)}, u32[]{:S(2)}) %all-to-all-start.1) | async-done | bytes 589856 | tf_op jit(solution)/shard_map/all_to_all | solution.py:81
  288.0 0.5 convert_reduce_fusion
  288.6 0.3 fusion.2
  288.8 0.6 slice_bitcast_fusion
  (18 shorter events, 0.1 us)
Async XLA Ops:
  7.2 2.3 copy-start
  7.2 28.0 %copy-start.2 = (bf16[64,6144]{1,0:T(8,128)(2,1)S(1)}, bf16[64,6144]{1,0:T(8,128)(2,1)}, u32[]{:S(2)}) copy-start(bf16[64,6144]{1,0:T(8,128)(2,1)} %param.13) | copy-start | bytes 2359300
  7.2 39.3 %copy-start.3 = (bf16[64,6144]{1,0:T(8,128)(2,1)S(1)}, bf16[64,6144]{1,0:T(8,128)(2,1)}, u32[]{:S(2)}) copy-start(bf16[64,6144]{1,0:T(8,128)(2,1)} %param.14) | copy-start | bytes 2359300
  7.2 47.3 %copy-start.5 = (s32[4]{0:T(128)S(1)}, s32[4]{0:T(128)}, u32[]{:S(2)}) copy-start(s32[4]{0:T(128)} %param.11) | copy-start | bytes 52
  7.2 47.9 %copy-start.4 = (s32[4]{0:T(128)S(1)}, s32[4]{0:T(128)}, u32[]{:S(2)}) copy-start(s32[4]{0:T(128)} %param.12) | copy-start | bytes 52
  7.2 74.0 %all-gather.2.cloned.1.call-start = ((), (), s32[]{:S(2)}) async-start(), calls=%async_computation.2 | async-start | bytes 5013504 | tf_op jit(solution)/shard_map/all_gather | solution.py:41
  35.1 69.7 %collective-permute-start = (bf16[64,6144]{1,0:T(8,128)(2,1)S(1)}, bf16[64,6144]{1,0:T(8,128)(2,1)}, u32[]{:S(2)}, u32[]{:S(2)}) collective-permute-start(bf16[64,6144]{1,0:T(8,128)(2,1)S(1)} %copy-done.2), channel_id=1, source_target_pairs={{0,128},{16,144},{32,160},{48,176},{64,192},{80,208},{96,224},{112... | collective-permute-start | bytes 2359304 | tf_op jit(solution)/shard_map/ppermute | solution.py:13
  38.0 74.0 %collective-permute-start.2 = (bf16[64,6144]{1,0:T(8,128)(2,1)S(1)}, bf16[64,6144]{1,0:T(8,128)(2,1)}, u32[]{:S(2)}, u32[]{:S(2)}) collective-permute-start(bf16[64,6144]{1,0:T(8,128)(2,1)S(1)} %copy-done.2), channel_id=1, source_target_pairs={{0,384},{16,400},{32,416},{48,432},{64,448},{80,464},{96,480},{112... | collective-permute-start | bytes 2359304 | tf_op jit(solution)/shard_map/ppermute | solution.py:13
  43.1 71.6 %collective-permute-start.1 = (bf16[64,6144]{1,0:T(8,128)(2,1)S(1)}, bf16[64,6144]{1,0:T(8,128)(2,1)}, u32[]{:S(2)}, u32[]{:S(2)}) collective-permute-start(bf16[64,6144]{1,0:T(8,128)(2,1)S(1)} %copy-done.2), channel_id=1, source_target_pairs={{0,256},{16,272},{32,288},{48,304},{64,320},{80,336},{96,352},{112... | collective-permute-start | bytes 2359304 | tf_op jit(solution)/shard_map/ppermute | solution.py:13
  46.5 169.8 %collective-permute-start.3 = (bf16[64,6144]{1,0:T(8,128)(2,1)S(1)}, bf16[64,6144]{1,0:T(8,128)(2,1)}, u32[]{:S(2)}, u32[]{:S(2)}) collective-permute-start(bf16[64,6144]{1,0:T(8,128)(2,1)S(1)} %copy-done.3), channel_id=1, source_target_pairs={{0,128},{16,144},{32,160},{48,176},{64,192},{80,208},{96,224},{112... | collective-permute-start | bytes 2359304 | tf_op jit(solution)/shard_map/ppermute | solution.py:13
  49.3 168.9 %collective-permute-start.5 = (bf16[64,6144]{1,0:T(8,128)(2,1)S(1)}, bf16[64,6144]{1,0:T(8,128)(2,1)}, u32[]{:S(2)}, u32[]{:S(2)}) collective-permute-start(bf16[64,6144]{1,0:T(8,128)(2,1)S(1)} %copy-done.3), channel_id=1, source_target_pairs={{0,384},{16,400},{32,416},{48,432},{64,448},{80,464},{96,480},{112... | collective-permute-start | bytes 2359304 | tf_op jit(solution)/shard_map/ppermute | solution.py:13
  81.2 4.1 %copy-start.1 = (bf16[384,6144]{1,0:T(8,128)(2,1)S(1)}, bf16[384,6144]{1,0:T(8,128)(2,1)}, u32[]{:S(2)}) copy-start(bf16[384,6144]{1,0:T(8,128)(2,1)} %all-gather.2.cloned.1.call-done) | copy-start | bytes 14155780
  85.3 26.1 %copy-start.7 = (bf16[1024,384]{1,0:T(8,128)(2,1)S(1)}, bf16[1024,384]{1,0:T(8,128)(2,1)}, u32[]{:S(2)}) copy-start(bf16[1024,384]{1,0:T(8,128)(2,1)} %param.15) | copy-start | bytes 2359300
  104.9 113.3 %collective-permute-start.4 = (bf16[64,6144]{1,0:T(8,128)(2,1)S(1)}, bf16[64,6144]{1,0:T(8,128)(2,1)}, u32[]{:S(2)}, u32[]{:S(2)}) collective-permute-start(bf16[64,6144]{1,0:T(8,128)(2,1)S(1)} %copy-done.3), channel_id=1, source_target_pairs={{0,256},{16,272},{32,288},{48,304},{64,320},{80,336},{96,352},{112... | collective-permute-start | bytes 2359304 | tf_op jit(solution)/shard_map/ppermute | solution.py:13
  112.0 106.2 %slice-start = ((s8[4718592]{0:T(1024)(128)(4,1)}), s8[524288]{0:T(1024)(128)(4,1)S(1)}, s32[]{:S(2)}) async-start(s8[4718592]{0:T(1024)(128)(4,1)} %bitcast.32), calls=%async_computation.3 | async-start | bytes 1048576
  112.1 128.9 %collective-permute-start.6 = (bf16[1024,384]{1,0:T(8,128)(2,1)}, bf16[1024,384]{1,0:T(8,128)(2,1)S(1)}, u32[]{:S(2)}, u32[]{:S(2)}) collective-permute-start(bf16[1024,384]{1,0:T(8,128)(2,1)} %param.15), channel_id=1, source_target_pairs={{0,128},{16,144},{32,160},{48,176},{64,192},{80,208},{96,224},{112... | collective-permute-start | bytes 2359304 | tf_op jit(solution)/shard_map/ppermute | solution.py:13
  114.7 126.3 %collective-permute-start.8 = (bf16[1024,384]{1,0:T(8,128)(2,1)}, bf16[1024,384]{1,0:T(8,128)(2,1)S(1)}, u32[]{:S(2)}, u32[]{:S(2)}) collective-permute-start(bf16[1024,384]{1,0:T(8,128)(2,1)} %param.15), channel_id=1, source_target_pairs={{0,384},{16,400},{32,416},{48,432},{64,448},{80,464},{96,480},{112... | collective-permute-start | bytes 2359304 | tf_op jit(solution)/shard_map/ppermute | solution.py:13
  120.2 96.1 %copy-start.8 = (bf16[1024,384]{1,0:T(8,128)(2,1)S(1)}, bf16[1024,384]{1,0:T(8,128)(2,1)}, u32[]{:S(2)}) copy-start(bf16[1024,384]{1,0:T(8,128)(2,1)} %param.15) | copy-start | bytes 2359300
  120.2 98.0 %slice-start.1 = ((s8[4718592]{0:T(1024)(128)(4,1)}), s8[4194304]{0:T(1024)(128)(4,1)S(1)}, s32[]{:S(2)}) async-start(s8[4718592]{0:T(1024)(128)(4,1)} %bitcast.32), calls=%async_computation.4 | async-start | bytes 8388608
  216.3 29.2 %collective-permute-start.7 = (bf16[1024,384]{1,0:T(8,128)(2,1)S(1)}, bf16[1024,384]{1,0:T(8,128)(2,1)S(1)}, u32[]{:S(2)}, u32[]{:S(2)}) collective-permute-start(bf16[1024,384]{1,0:T(8,128)(2,1)S(1)} %copy-done.8), channel_id=1, source_target_pairs={{0,256},{16,272},{32,288},{48,304},{64,320},{80,336},{96,352},{112... | collective-permute-start | bytes 2359304 | tf_op jit(solution)/shard_map/ppermute | solution.py:13
  249.2 21.9 %copy-start.6 = (s32[16,2]{0,1:T(2,128)S(1)}, s32[16,2]{0,1:T(2,128)}, u32[]{:S(2)}) copy-start(s32[16,2]{0,1:T(2,128)} %param.10) | copy-start | bytes 388
  250.6 37.4 %all-to-all-start.1 = ((bf16[2,32,12,384]{3,0,2,1:T(2,128)(2,1)}), bf16[2,32,12,384]{3,0,2,1:T(2,128)(2,1)S(1)}, u32[]{:S(2)}, u32[]{:S(2)}) async-start(bf16[2,32,12,384]{3,0,2,1:T(2,128)(2,1)} %copy.28), calls=%async_computation.1 | async-start | bytes 1179648 | tf_op jit(solution)/shard_map/all_to_all | solution.py:81
Sparse Core Ops, SparseCore 0:
  35.2 45.9 all-gather.1
where the time goes:
time: 297 us; the launch traced here: 296 us
  waiting for transfers between devices  132 us (44%)
  blocking collectives  59.5 us (20%)
  starting transfers between devices  56.2 us (19%)
  matrix products  23.7 us (8%)
  between operations  14.5 us (5%)
  other arithmetic  5.73 us (2%)
  local copies, waits for them, and re-layouts  4.15 us (1%)
    ppermute x9, waiting for transfers between devices, passed_along(): lax.ppermute(value, axis, [(i, (i + by) % devices) for i in range(devices)])  92.8 us
    ppermute x9, starting transfers between devices, passed_along(): lax.ppermute(value, axis, [(i, (i + by) % devices) for i in range(devices)])  35.7 us
    all_gather x2, blocking collectives, project(): units = lax.all_gather(hidden, 'exp', axis=1, tiled=True)  34.8 us
    all_to_all x1, blocking collectives, local(): lax.all_to_all(copies, 'tok', split_axis=0, concat_axis=0, tiled=True)  24.7 us
    all_gather x1, waiting for transfers between devices, local(): rows = lax.all_gather(rows_part, 'exp', axis=1, tiled=True)  22.8 us
    all_to_all x1, starting transfers between devices, local(): lax.all_to_all(stacked.astype(jnp.bfloat16), 'tok', split_axis=1, concat_...  20.4 us
    all_to_all x1, waiting for transfers between devices, local(): lax.all_to_all(stacked.astype(jnp.bfloat16), 'tok', split_axis=1, concat_...  16.8 us
    dot_general x2, matrix products, project(): jnp.einsum('sd,fd->sf', rows, gate_w, preferred_element_type=jnp.float32)  11.7 us
  transfers between devices with their start and end apart: 11, of which 4 were waited for; matrix products, arithmetic and copies ran while one was open for 8% of the time, Pallas kernels for 0%

commit v1 on v0

--- a/solution.py
+++ b/solution.py
@@ -44,7 +44,9 @@
         gate = jnp.einsum("sd,fd->sf", rows, gate_w, preferred_element_type=jnp.float32)
         upper = jnp.einsum("sd,fd->sf", rows, up_w, preferred_element_type=jnp.float32)
         hidden = (jax.nn.silu(gate) * upper).astype(jnp.bfloat16)
-        units = lax.all_gather(hidden, "exp", axis=1, tiled=True)
+        units = jnp.concatenate(
+            lax.all_to_all(jnp.stack([hidden] * lax.axis_size("exp")), "exp", 0, 0), axis=1
+        )
         return jnp.dot(units, down_w, preferred_element_type=jnp.float32)
 
     first = project(w_gate, w_up, w_down)

time: 297 us -> 314 us (1.057)
  starting transfers between devices: 56.2 us -> 99.4 us
  blocking collectives: 59.5 us -> 24.7 us
  local copies, waits for them, and re-layouts: 4.15 us -> 11.8 us
  matrix products: 23.7 us -> 27.1 us
    all_to_all x0 -> x2, starting transfers between devices: none -> 36 us  [project(): lax.all_to_all(jnp.stack([hidden] * lax.axis_size('exp')), 'exp', 0, 0)]
    all_gather x2 -> x0, blocking collectives: 34.8 us -> none  [project(): units = lax.all_gather(hidden, 'exp', axis=1, tiled=True)]
    ppermute x9, waiting for transfers between devices: 92.8 us -> 72.2 us  [passed_along(): lax.ppermute(value, axis, [(i, (i + by) % devices) for i in range(devices)])]
    all_gather x1, waiting for transfers between devices: 22.8 us -> 34.6 us  [local(): rows = lax.all_gather(rows_part, 'exp', axis=1, tiled=True)]
    another operation x0 -> x4, local copies, waits for them, and re-layouts: none -> 5.23 us
    all_to_all x0 -> x2, waiting for transfers between devices: none -> 5.12 us  [project(): lax.all_to_all(jnp.stack([hidden] * lax.axis_size('exp')), 'exp', 0, 0)]
    all_to_all x1, starting transfers between devices: 20.4 us -> 25.5 us  [local(): lax.all_to_all(stacked.astype(jnp.bfloat16), 'tok', split_axis=1, concat_...]
    dot_general x2, matrix products: 4.13 us -> 7.7 us  [project(): return jnp.dot(units, down_w, preferred_element_type=jnp.float32)]
  transfers between devices with their start and end apart: 11 -> 13, of which waited for: 4 -> 7; matrix products, arithmetic and copies ran while one was open for 8% -> 10% of each run, Pallas kernels for 0% -> 0%
where the time goes in v1:
time: 314 us
  waiting for transfers between devices  131 us (42%)
  starting transfers between devices  99.4 us (32%)
  matrix products  27.1 us (9%)
  blocking collectives  24.7 us (8%)
  between operations  14.4 us (5%)
  local copies, waits for them, and re-layouts  11.8 us (4%)
  other arithmetic  5.6 us (2%)
    ppermute x9, waiting for transfers between devices, passed_along(): lax.ppermute(value, axis, [(i, (i + by) % devices) for i in range(devices)])  72.2 us
    ppermute x9, starting transfers between devices, passed_along(): lax.ppermute(value, axis, [(i, (i + by) % devices) for i in range(devices)])  37.9 us
    all_to_all x2, starting transfers between devices, project(): lax.all_to_all(jnp.stack([hidden] * lax.axis_size('exp')), 'exp', 0, 0)  36 us
    all_gather x1, waiting for transfers between devices, local(): rows = lax.all_gather(rows_part, 'exp', axis=1, tiled=True)  34.6 us
    all_to_all x1, starting transfers between devices, local(): lax.all_to_all(stacked.astype(jnp.bfloat16), 'tok', split_axis=1, concat_...  25.5 us
    all_to_all x1, blocking collectives, local(): lax.all_to_all(copies, 'tok', split_axis=0, concat_axis=0, tiled=True)  24.7 us
    all_to_all x1, waiting for transfers between devices, local(): lax.all_to_all(stacked.astype(jnp.bfloat16), 'tok', split_axis=1, concat_...  18.5 us
    dot_general x2, matrix products, project(): jnp.einsum('sd,fd->sf', rows, gate_w, preferred_element_type=jnp.float32)  11.6 us
  transfers between devices with their start and end apart: 13, of which 7 were waited for; matrix products, arithmetic and copies ran while one was open for 10% of the time, Pallas kernels for 0%

profile of v1, /device:TPU:8, one launch (start us, length us, event | category | flops | bytes accessed | tf_op | source)
XLA Modules:
  0.0 313.5 jit_solution(3861222236888419442)
XLA Ops:
  7.2 0.0 copy-start
  7.2 0.0 all-gather.2.cloned.1.call-start
  7.2 0.7 fusion.31
  8.0 0.8 copy.42
  8.7 0.1 eq.85
  8.8 0.1 fusion.29
  8.9 0.1 reduce_window_sum.11
  9.0 0.2 select_reduce_fusion
  9.1 0.1 eq.89
  9.2 0.1 copy.43
  9.4 0.1 convolution_convert_fusion.2
  9.6 24.7 %all_to_all.20 = bf16[32,12,384]{2,1,0:T(8,128)(2,1)S(1)} all-to-all(bf16[32,12,384]{2,1,0:T(8,128)(2,1)S(1)} %bitcast.45), channel_id=1, replica_groups=mesh['tok'=32,'exp'=16] {'tok'}, dimensions={0} | all-to-all | bytes 589824 | tf_op jit(solution)/shard_map/all_to_all | solution.py:39
  34.2 0.8 reshape.103
  35.0 0.0 all-gather.2.cloned.1.call-update
  35.1 0.0 copy-start.3
  35.1 3.0 collective-permute-start
  38.1 5.1 %collective-permute-start.2 = (bf16[64,6144]{1,0:T(8,128)(2,1)S(1)}, bf16[64,6144]{1,0:T(8,128)(2,1)}, u32[]{:S(2)}, u32[]{:S(2)}) collective-permute-start(bf16[64,6144]{1,0:T(8,128)(2,1)S(1)} %copy-done.2), channel_id=1, source_target_pairs={{0,384},{16,400},{32,416},{48,432},{64,448},{80,464},{96,480},{112... | collective-permute-start | bytes 2359304 | tf_op jit(solution)/shard_map/ppermute | solution.py:13
  43.2 3.3 %collective-permute-start.1 = (bf16[64,6144]{1,0:T(8,128)(2,1)S(1)}, bf16[64,6144]{1,0:T(8,128)(2,1)}, u32[]{:S(2)}, u32[]{:S(2)}) collective-permute-start(bf16[64,6144]{1,0:T(8,128)(2,1)S(1)} %copy-done.2), channel_id=1, source_target_pairs={{0,256},{16,272},{32,288},{48,304},{64,320},{80,336},{96,352},{112... | collective-permute-start | bytes 2359304 | tf_op jit(solution)/shard_map/ppermute | solution.py:13
  46.5 34.6 %all-gather.2.cloned.1.call-done = bf16[384,6144]{1,0:T(8,128)(2,1)} async-done(((bf16[384,384]{1,0:T(8,128)(2,1)}), bf16[384,6144]{1,0:T(8,128)(2,1)}) %all-gather.2.cloned.1.call-update) | async-done | bytes 4718608 | tf_op jit(solution)/shard_map/all_gather | solution.py:41
  81.1 4.1 %fusion.38 = f32[384,64]{0,1:T(8,128)S(1)} fusion(bf16[384,6144]{1,0:T(8,128)(2,1)} %all-gather.2.cloned.1.call-done, bf16[64,6144]{1,0:T(8,128)(2,1)S(1)} %copy-done.2), kind=kOutput, calls=%fused_computation.64 | convolution fusion | flops 301989888 | bytes 5603328 | tf_op jit(solution)/shard_map/sd,fd->sf/dot_general | solution.py:44
  85.2 1.6 fusion.2
  86.8 0.0 copy-start.5
  86.8 0.0 copy-start.4
  86.8 1.0 stack.7
  87.8 4.4 %all-to-all-start.1 = ((bf16[16,384,64]{1,2,0:T(8,128)(2,1)}), bf16[16,384,64]{1,2,0:T(8,128)(2,1)S(1)}, u32[]{:S(2)}, u32[]{:S(2)}) async-start(bf16[16,384,64]{1,2,0:T(8,128)(2,1)} %stack.7), calls=%async_computation.1 | async-start | bytes 1572864 | tf_op jit(solution)/shard_map/all_to_all | solution.py:48
  92.2 4.3 %collective-permute-start.3 = (bf16[64,6144]{1,0:T(8,128)(2,1)S(1)}, bf16[64,6144]{1,0:T(8,128)(2,1)}, u32[]{:S(2)}, u32[]{:S(2)}) collective-permute-start(bf16[64,6144]{1,0:T(8,128)(2,1)S(1)} %copy-done.3), channel_id=1, source_target_pairs={{0,128},{16,144},{32,160},{48,176},{64,192},{80,208},{96,224},{112... | collective-permute-start | bytes 2359304 | tf_op jit(solution)/shard_map/ppermute | solution.py:13
  96.6 3.6 %collective-permute-start.5 = (bf16[64,6144]{1,0:T(8,128)(2,1)S(1)}, bf16[64,6144]{1,0:T(8,128)(2,1)}, u32[]{:S(2)}, u32[]{:S(2)}) collective-permute-start(bf16[64,6144]{1,0:T(8,128)(2,1)S(1)} %copy-done.3), channel_id=1, source_target_pairs={{0,384},{16,400},{32,416},{48,432},{64,448},{80,464},{96,480},{112... | collective-permute-start | bytes 2359304 | tf_op jit(solution)/shard_map/ppermute | solution.py:13
  100.2 0.0 collective-permute-done
  100.2 6.4 %collective-permute-start.4 = (bf16[64,6144]{1,0:T(8,128)(2,1)S(1)}, bf16[64,6144]{1,0:T(8,128)(2,1)}, u32[]{:S(2)}, u32[]{:S(2)}) collective-permute-start(bf16[64,6144]{1,0:T(8,128)(2,1)S(1)} %copy-done.3), channel_id=1, source_target_pairs={{0,256},{16,272},{32,288},{48,304},{64,320},{80,336},{96,352},{112... | collective-permute-start | bytes 2359304 | tf_op jit(solution)/shard_map/ppermute | solution.py:13
  106.7 0.6 fusion.32
  107.3 1.2 fusion.37
  108.5 2.0 fusion.33
  110.5 0.0 collective-permute-done.2
  110.5 3.2 %collective-permute-done.1 = bf16[64,6144]{1,0:T(8,128)(2,1)} collective-permute-done((bf16[64,6144]{1,0:T(8,128)(2,1)S(1)}, bf16[64,6144]{1,0:T(8,128)(2,1)}, u32[]{:S(2)}, u32[]{:S(2)}) %collective-permute-start.1) | collective-permute-done | bytes 786464 | tf_op jit(solution)/shard_map/ppermute | solution.py:13
  113.7 7.5 %fusion.5 = f32[384,64]{0,1:T(8,128)S(1)} fusion(bf16[384,6144]{1,0:T(8,128)(2,1)} %all-gather.2.cloned.1.call-done, bf16[64,6144]{1,0:T(8,128)(2,1)} %collective-permute-done.2, bf16[64,6144]{1,0:T(8,128)(2,1)} %collective-permute-done.1, bf16[64,6144]{1,0:T(8,128)(2,1)} %collective-permute-done, bf16[64,6144]{1,0:T(8,128)(2,1)S(1)} %copy-done.2, ...), kind=kOutput, calls=%fused_computation.14 | convolution fusion | flops 306708480 | bytes 7962640 | tf_op jit(solution)/shard_map/sd,fd->sf/dot_general | solution.py:44
  121.3 38.6 %collective-permute-done.3 = bf16[64,6144]{1,0:T(8,128)(2,1)} collective-permute-done((bf16[64,6144]{1,0:T(8,128)(2,1)S(1)}, bf16[64,6144]{1,0:T(8,128)(2,1)}, u32[]{:S(2)}, u32[]{:S(2)}) %collective-permute-start.3) | collective-permute-done | bytes 786464 | tf_op jit(solution)/shard_map/ppermute | solution.py:13
  159.8 0.0 collective-permute-done.5
  159.9 0.0 collective-permute-done.4
  159.9 5.9 %multiply_convert_fusion = bf16[384,64]{0,1:T(8,128)(2,1)S(1)} fusion(f32[384,64]{0,1:T(8,128)S(1)} %fusion.5, bf16[384,6144]{1,0:T(8,128)(2,1)S(1)} %bitcast.42, bf16[64,6144]{1,0:T(8,128)(2,1)} %collective-permute-done.5, bf16[64,6144]{1,0:T(8,128)(2,1)} %collective-permute-done.4, bf16[64,6144]{1,0:T(8,128)(2,1)} %collective-permute-done.3, ...), kind=kOutput, calls=%fused_computation.34 | convolution fusion | flops 306855936 | bytes 8011792 | tf_op jit(solution)/shard_map/sd,fd->sf/dot_general | solution.py:45
  165.8 0.0 all-to-all-done.1
  165.8 1.0 stack.8
  166.8 31.6 %all-to-all-start.2 = ((bf16[16,384,64]{1,2,0:T(8,128)(2,1)}), bf16[16,384,64]{1,2,0:T(8,128)(2,1)S(1)}, u32[]{:S(2)}, u32[]{:S(2)}) async-start(bf16[16,384,64]{1,2,0:T(8,128)(2,1)} %stack.8), calls=%async_computation.2 | async-start | bytes 1572864 | tf_op jit(solution)/shard_map/all_to_all | solution.py:48
  198.4 2.3 collective-permute-start.6
  200.6 5.7 %collective-permute-start.8 = (bf16[1024,384]{1,0:T(8,128)(2,1)}, bf16[1024,384]{1,0:T(8,128)(2,1)}, u32[]{:S(2)}, u32[]{:S(2)}) collective-permute-start(bf16[1024,384]{1,0:T(8,128)(2,1)} %param.15), channel_id=1, source_target_pairs={{0,384},{16,400},{32,416},{48,432},{64,448},{80,464},{96,480},{112... | collective-permute-start | bytes 2359304 | tf_op jit(solution)/shard_map/ppermute | solution.py:13
  206.3 4.2 %collective-permute-start.7 = (bf16[1024,384]{1,0:T(8,128)(2,1)}, bf16[1024,384]{1,0:T(8,128)(2,1)}, u32[]{:S(2)}, u32[]{:S(2)}) collective-permute-start(bf16[1024,384]{1,0:T(8,128)(2,1)} %param.15), channel_id=1, source_target_pairs={{0,256},{16,272},{32,288},{48,304},{64,320},{80,336},{96,352},{112... | collective-permute-start | bytes 2359304 | tf_op jit(solution)/shard_map/ppermute | solution.py:13
  210.5 1.3 copy.45
  211.8 2.0 reshape.105
  213.8 5.1 %all-to-all-done.2 = bf16[16,384,64]{1,2,0:T(8,128)(2,1)S(1)} async-done(((bf16[16,384,64]{1,2,0:T(8,128)(2,1)}), bf16[16,384,64]{1,2,0:T(8,128)(2,1)S(1)}, u32[]{:S(2)}, u32[]{:S(2)}) %all-to-all-start.2) | async-done | bytes 786464 | tf_op jit(solution)/shard_map/all_to_all | solution.py:48
  219.0 1.3 copy.47
  220.2 1.2 reshape.107
  221.5 2.1 fusion
  223.5 26.9 %collective-permute-done.6 = bf16[1024,384]{1,0:T(8,128)(2,1)} collective-permute-done((bf16[1024,384]{1,0:T(8,128)(2,1)}, bf16[1024,384]{1,0:T(8,128)(2,1)}, u32[]{:S(2)}, u32[]{:S(2)}) %collective-permute-start.6) | collective-permute-done | bytes 786464 | tf_op jit(solution)/shard_map/ppermute | solution.py:13
  250.5 0.0 collective-permute-done.8
  250.5 3.5 %collective-permute-done.7 = bf16[1024,384]{1,0:T(8,128)(2,1)} collective-permute-done((bf16[1024,384]{1,0:T(8,128)(2,1)}, bf16[1024,384]{1,0:T(8,128)(2,1)}, u32[]{:S(2)}, u32[]{:S(2)}) %collective-permute-start.7) | collective-permute-done | bytes 786464 | tf_op jit(solution)/shard_map/ppermute | solution.py:13
  254.0 5.6 %fusion.1 = bf16[1,32,12,384]{3,1,2,0:T(8,128)(2,1)S(1)} fusion(bf16[1024,384]{1,0:T(8,128)(2,1)} %collective-permute-done.8, bf16[1024,384]{1,0:T(8,128)(2,1)} %collective-permute-done.7, bf16[1024,384]{1,0:T(8,128)(2,1)} %collective-permute-done.6, bf16[1024,384]{1,0:T(8,128)(2,1)} %param.15, bf16[32,12,1024]{2,1,0:T(8,128)(2,1)S(1)} %reshape.107, ...), kind=kOutput, calls=%fused_computation.7 | convolution fusion | flops 306855936 | bytes 4227088 | tf_op jit(solution)/shard_map/dot_general | solution.py:50
  259.6 0.0 copy-start.6
  259.6 0.1 pad_maximum_fusion
  259.7 1.4 copy.49
  261.1 25.5 %all-to-all-start.3 = ((bf16[2,32,12,384]{3,0,2,1:T(2,128)(2,1)}), bf16[2,32,12,384]{3,0,2,1:T(2,128)(2,1)S(1)}, u32[]{:S(2)}, u32[]{:S(2)}) async-start(bf16[2,32,12,384]{3,0,2,1:T(2,128)(2,1)} %copy.49), calls=%async_computation.3 | async-start | bytes 1179648 | tf_op jit(solution)/shard_map/all_to_all | solution.py:83
  286.6 0.1 copy.52
  286.7 18.5 %all-to-all-done.3 = bf16[2,32,12,384]{3,0,2,1:T(2,128)(2,1)S(1)} async-done(((bf16[2,32,12,384]{3,0,2,1:T(2,128)(2,1)}), bf16[2,32,12,384]{3,0,2,1:T(2,128)(2,1)S(1)}, u32[]{:S(2)}, u32[]{:S(2)}) %all-to-all-start.3) | async-done | bytes 589856 | tf_op jit(solution)/shard_map/all_to_all | solution.py:83
  305.3 0.5 convert_reduce_fusion
  305.8 0.3 fusion.4
  306.1 0.6 slice_bitcast_fusion
  (20 shorter events, 0.1 us)
Async XLA Ops:
  7.2 2.2 copy-start
  7.2 27.9 %copy-start.2 = (bf16[64,6144]{1,0:T(8,128)(2,1)S(1)}, bf16[64,6144]{1,0:T(8,128)(2,1)}, u32[]{:S(2)}) copy-start(bf16[64,6144]{1,0:T(8,128)(2,1)} %param.13) | copy-start | bytes 2359300
  7.2 73.9 %all-gather.2.cloned.1.call-start = ((), (), s32[]{:S(2)}) async-start(), calls=%async_computation.4 | async-start | bytes 5013504 | tf_op jit(solution)/shard_map/all_gather | solution.py:41
  35.1 50.1 %copy-start.3 = (bf16[64,6144]{1,0:T(8,128)(2,1)S(1)}, bf16[64,6144]{1,0:T(8,128)(2,1)}, u32[]{:S(2)}) copy-start(bf16[64,6144]{1,0:T(8,128)(2,1)} %param.14) | copy-start | bytes 2359300
  35.1 65.2 %collective-permute-start = (bf16[64,6144]{1,0:T(8,128)(2,1)S(1)}, bf16[64,6144]{1,0:T(8,128)(2,1)}, u32[]{:S(2)}, u32[]{:S(2)}) collective-permute-start(bf16[64,6144]{1,0:T(8,128)(2,1)S(1)} %copy-done.2), channel_id=1, source_target_pairs={{0,128},{16,144},{32,160},{48,176},{64,192},{80,208},{96,224},{112... | collective-permute-start | bytes 2359304 | tf_op jit(solution)/shard_map/ppermute | solution.py:13
  38.1 72.4 %collective-permute-start.2 = (bf16[64,6144]{1,0:T(8,128)(2,1)S(1)}, bf16[64,6144]{1,0:T(8,128)(2,1)}, u32[]{:S(2)}, u32[]{:S(2)}) collective-permute-start(bf16[64,6144]{1,0:T(8,128)(2,1)S(1)} %copy-done.2), channel_id=1, source_target_pairs={{0,384},{16,400},{32,416},{48,432},{64,448},{80,464},{96,480},{112... | collective-permute-start | bytes 2359304 | tf_op jit(solution)/shard_map/ppermute | solution.py:13
  43.2 70.5 %collective-permute-start.1 = (bf16[64,6144]{1,0:T(8,128)(2,1)S(1)}, bf16[64,6144]{1,0:T(8,128)(2,1)}, u32[]{:S(2)}, u32[]{:S(2)}) collective-permute-start(bf16[64,6144]{1,0:T(8,128)(2,1)S(1)} %copy-done.2), channel_id=1, source_target_pairs={{0,256},{16,272},{32,288},{48,304},{64,320},{80,336},{96,352},{112... | collective-permute-start | bytes 2359304 | tf_op jit(solution)/shard_map/ppermute | solution.py:13
  81.1 4.1 %copy-start.1 = (bf16[384,6144]{1,0:T(8,128)(2,1)S(1)}, bf16[384,6144]{1,0:T(8,128)(2,1)}, u32[]{:S(2)}) copy-start(bf16[384,6144]{1,0:T(8,128)(2,1)} %all-gather.2.cloned.1.call-done) | copy-start | bytes 14155780
  86.8 19.9 %copy-start.5 = (s32[4]{0:T(128)S(1)}, s32[4]{0:T(128)}, u32[]{:S(2)}) copy-start(s32[4]{0:T(128)} %param.11) | copy-start | bytes 52
  86.8 20.5 %copy-start.4 = (s32[4]{0:T(128)S(1)}, s32[4]{0:T(128)}, u32[]{:S(2)}) copy-start(s32[4]{0:T(128)} %param.12) | copy-start | bytes 52
  87.8 72.1 %slice-start = ((s8[4718592]{0:T(1024)(128)(4,1)}), s8[524288]{0:T(1024)(128)(4,1)S(1)}, s32[]{:S(2)}) async-start(s8[4718592]{0:T(1024)(128)(4,1)} %bitcast.41), calls=%async_computation.5 | async-start | bytes 1048576
  87.8 78.0 %all-to-all-start.1 = ((bf16[16,384,64]{1,2,0:T(8,128)(2,1)}), bf16[16,384,64]{1,2,0:T(8,128)(2,1)S(1)}, u32[]{:S(2)}, u32[]{:S(2)}) async-start(bf16[16,384,64]{1,2,0:T(8,128)(2,1)} %stack.7), calls=%async_computation.1 | async-start | bytes 1572864 | tf_op jit(solution)/shard_map/all_to_all | solution.py:48
  92.2 67.6 %collective-permute-start.3 = (bf16[64,6144]{1,0:T(8,128)(2,1)S(1)}, bf16[64,6144]{1,0:T(8,128)(2,1)}, u32[]{:S(2)}, u32[]{:S(2)}) collective-permute-start(bf16[64,6144]{1,0:T(8,128)(2,1)S(1)} %copy-done.3), channel_id=1, source_target_pairs={{0,128},{16,144},{32,160},{48,176},{64,192},{80,208},{96,224},{112... | collective-permute-start | bytes 2359304 | tf_op jit(solution)/shard_map/ppermute | solution.py:13
  96.6 63.3 %collective-permute-start.5 = (bf16[64,6144]{1,0:T(8,128)(2,1)S(1)}, bf16[64,6144]{1,0:T(8,128)(2,1)}, u32[]{:S(2)}, u32[]{:S(2)}) collective-permute-start(bf16[64,6144]{1,0:T(8,128)(2,1)S(1)} %copy-done.3), channel_id=1, source_target_pairs={{0,384},{16,400},{32,416},{48,432},{64,448},{80,464},{96,480},{112... | collective-permute-start | bytes 2359304 | tf_op jit(solution)/shard_map/ppermute | solution.py:13
  100.2 59.6 %collective-permute-start.4 = (bf16[64,6144]{1,0:T(8,128)(2,1)S(1)}, bf16[64,6144]{1,0:T(8,128)(2,1)}, u32[]{:S(2)}, u32[]{:S(2)}) collective-permute-start(bf16[64,6144]{1,0:T(8,128)(2,1)S(1)} %copy-done.3), channel_id=1, source_target_pairs={{0,256},{16,272},{32,288},{48,304},{64,320},{80,336},{96,352},{112... | collective-permute-start | bytes 2359304 | tf_op jit(solution)/shard_map/ppermute | solution.py:13
  113.7 46.1 %slice-start.1 = ((s8[4718592]{0:T(1024)(128)(4,1)}), s8[4194304]{0:T(1024)(128)(4,1)S(1)}, s32[]{:S(2)}) async-start(s8[4718592]{0:T(1024)(128)(4,1)} %bitcast.41), calls=%async_computation.6 | async-start | bytes 8388608
  166.8 52.2 %all-to-all-start.2 = ((bf16[16,384,64]{1,2,0:T(8,128)(2,1)}), bf16[16,384,64]{1,2,0:T(8,128)(2,1)S(1)}, u32[]{:S(2)}, u32[]{:S(2)}) async-start(bf16[16,384,64]{1,2,0:T(8,128)(2,1)} %stack.8), calls=%async_computation.2 | async-start | bytes 1572864 | tf_op jit(solution)/shard_map/all_to_all | solution.py:48
  198.4 52.1 %collective-permute-start.6 = (bf16[1024,384]{1,0:T(8,128)(2,1)}, bf16[1024,384]{1,0:T(8,128)(2,1)}, u32[]{:S(2)}, u32[]{:S(2)}) collective-permute-start(bf16[1024,384]{1,0:T(8,128)(2,1)} %param.15), channel_id=1, source_target_pairs={{0,128},{16,144},{32,160},{48,176},{64,192},{80,208},{96,224},{112... | collective-permute-start | bytes 2359304 | tf_op jit(solution)/shard_map/ppermute | solution.py:13
  200.6 49.8 %collective-permute-start.8 = (bf16[1024,384]{1,0:T(8,128)(2,1)}, bf16[1024,384]{1,0:T(8,128)(2,1)}, u32[]{:S(2)}, u32[]{:S(2)}) collective-permute-start(bf16[1024,384]{1,0:T(8,128)(2,1)} %param.15), channel_id=1, source_target_pairs={{0,384},{16,400},{32,416},{48,432},{64,448},{80,464},{96,480},{112... | collective-permute-start | bytes 2359304 | tf_op jit(solution)/shard_map/ppermute | solution.py:13
  206.3 47.6 %collective-permute-start.7 = (bf16[1024,384]{1,0:T(8,128)(2,1)}, bf16[1024,384]{1,0:T(8,128)(2,1)}, u32[]{:S(2)}, u32[]{:S(2)}) collective-permute-start(bf16[1024,384]{1,0:T(8,128)(2,1)} %param.15), channel_id=1, source_target_pairs={{0,256},{16,272},{32,288},{48,304},{64,320},{80,336},{96,352},{112... | collective-permute-start | bytes 2359304 | tf_op jit(solution)/shard_map/ppermute | solution.py:13
  259.6 27.0 %copy-start.6 = (s32[16,2]{0,1:T(2,128)S(1)}, s32[16,2]{0,1:T(2,128)}, u32[]{:S(2)}) copy-start(s32[16,2]{0,1:T(2,128)} %param.10) | copy-start | bytes 388
  261.1 44.1 %all-to-all-start.3 = ((bf16[2,32,12,384]{3,0,2,1:T(2,128)(2,1)}), bf16[2,32,12,384]{3,0,2,1:T(2,128)(2,1)S(1)}, u32[]{:S(2)}, u32[]{:S(2)}) async-start(bf16[2,32,12,384]{3,0,2,1:T(2,128)(2,1)} %copy.49), calls=%async_computation.3 | async-start | bytes 1179648 | tf_op jit(solution)/shard_map/all_to_all | solution.py:83
Sparse Core Ops, SparseCore 0:
  35.2 45.9 all-gather.1
